TPU v7x, 256 devices: a whole 4x4x8 slice. The times are simulated.
256 devices in a mesh: tok: 64 (over x, z, core), ch: 4 (over y).
Axes of the slice: x: 4, y: 4, z: 8, core: 2. Of those that a mesh axis runs over, the one named last changes fastest.
Arguments:
- inputs: float32 [65536, 1024], P('tok', 'ch'), may hold values from -6 to 6
- factor_one: float32 [512, 512], replicated, may hold values from -0.25 to 0.25
- twiddle: float32 [128, 512], P('tok'), may hold values from -4 to 4
- factor_two: float32 [128, 128], replicated, may hold values from -0.5 to 0.5
- w_up: bfloat16 [4, 256, 1024], P('ch', 'tok'), may hold values from -0.375 to 0.375
- w_down: bfloat16 [4, 1024, 256], P('ch', 'tok'), may hold values from -0.1875 to 0.1875
- out_cotangent: float32 [65536, 1024], P('tok', 'ch'), may hold values from -6 to 6
Outputs:
- outputs: float32 [65536, 1024], P('tok', 'ch')
- grad_inputs: float32 [65536, 1024], P('tok', 'ch')
- grad_factor_one: float32 [512, 512], replicated
- grad_factor_two: float32 [128, 128], replicated
- grad_up: float32 [4, 256, 1024], P('ch', 'tok')
- grad_down: float32 [4, 1024, 256], P('ch', 'tok')
All inputs are finite; a program needn't handle non-finite values.
Results may differ from a plain program's by a relative error of at most 0.0057.
Values may be sent and summed in bfloat16 or wider, within the bound.
A program may use at most 64 MiB of HBM per device.

v0:
```python
import math
import jax
import jax.numpy as jnp
from jax import lax
from jax.sharding import PartitionSpec as P

inv_root_two = 1.0 / math.sqrt(2.0)
inv_root_tau = 1.0 / math.sqrt(2.0 * math.pi)


def gelu_parts(value):
    cdf = 0.5 * (1.0 + jax.scipy.special.erf(value * inv_root_two))
    return (value * cdf, cdf + value * jnp.exp(-0.5 * value * value) * inv_root_tau)


def to_columns(block):
    count = lax.axis_size("tok")
    rows, width, chans = block.shape
    return lax.all_to_all(
        block.reshape(rows, count, width // count, chans),
        "tok",
        split_axis=1,
        concat_axis=0,
        tiled=True,
    ).reshape(count * rows, width // count, chans)


def to_rows(block):
    return lax.all_to_all(block, "tok", split_axis=0, concat_axis=1, tiled=True)


def local(inputs, factor_one, twiddle, factor_two, w_up, w_down, out_cotangent):
    high = lax.Precision.HIGHEST
    rows = twiddle.shape[0]
    width = twiddle.shape[1]
    chans = inputs.shape[1]
    panels = (
        lax.all_gather(w_up, "tok", axis=1, tiled=True),
        lax.all_gather(w_down, "tok", axis=1, tiled=True),
    )
    up_w = panels[0][0]
    down_w = panels[1][0]
    grid = inputs.reshape(rows, width, chans)
    first = jnp.einsum("kj,ijc->ikc", factor_one, grid, precision=high)
    mid = first * twiddle[:, :, None]
    mid_cols = to_columns(mid)
    mixed_cols = jnp.einsum("mi,ikc->mkc", factor_two, mid_cols, precision=high)
    mixed = to_rows(mixed_cols).reshape(rows * width, chans)
    gate = jax.nn.sigmoid(inputs)
    branch = inputs + gate * mixed
    normed = branch.astype(jnp.bfloat16)
    up = jnp.dot(normed, up_w, preferred_element_type=jnp.float32)
    active, slope = gelu_parts(up)
    hidden = active.astype(jnp.bfloat16)
    outputs = branch + jnp.dot(hidden, down_w, preferred_element_type=jnp.float32)
    cot = out_cotangent.astype(jnp.bfloat16)
    d_hidden = jnp.dot(cot, down_w.T, preferred_element_type=jnp.float32)
    d_up = (d_hidden * slope).astype(jnp.bfloat16)
    d_branch = out_cotangent + jnp.dot(d_up, up_w.T, preferred_element_type=jnp.float32)
    grad_down_part = jnp.dot(hidden.T, cot, preferred_element_type=jnp.float32)
    grad_up_part = jnp.dot(normed.T, d_up, preferred_element_type=jnp.float32)
    grad_up, grad_down = (
        lax.psum_scatter(grad_up_part[None], "tok", scatter_dimension=1, tiled=True),
        lax.psum_scatter(grad_down_part[None], "tok", scatter_dimension=1, tiled=True),
    )
    d_mixed = d_branch * gate
    direct = d_branch * (1.0 + gate * (1.0 - gate) * mixed)
    cot_cols = to_columns(d_mixed.reshape(rows, width, chans))
    d_mid_cols = jnp.einsum("mi,mkc->ikc", factor_two, cot_cols, precision=high)
    two_part = jnp.einsum("mkc,ikc->mi", cot_cols, mid_cols, precision=high)
    d_first = to_rows(d_mid_cols) * twiddle[:, :, None]
    one_part = jnp.einsum("ikc,ijc->kj", d_first, grid, precision=high)
    d_grid = jnp.einsum("kj,ikc->ijc", factor_one, d_first, precision=high)
    grad_inputs = direct + d_grid.reshape(rows * width, chans)
    grad_one, grad_two = lax.psum((one_part, two_part), ("tok", "ch"))
    return (outputs, grad_inputs, grad_one, grad_two, grad_up, grad_down)


def solution(mesh):
    in_specs = (
        P("tok", "ch"),
        P(),
        P("tok", None),
        P(),
        P("ch", "tok", None),
        P("ch", "tok", None),
        P("tok", "ch"),
    )
    out_specs = (
        P("tok", "ch"),
        P("tok", "ch"),
        P(),
        P(),
        P("ch", "tok", None),
        P("ch", "tok", None),
    )
    return jax.shard_map(local, mesh=mesh, in_specs=in_specs, out_specs=out_specs, check_vma=False)
```

profile of v0, /device:TPU:4, one launch (start us, length us, event | category | flops | bytes accessed | tf_op | source)
XLA Modules:
  0.0 719.0 jit_solution(10194359381156684317)
XLA Ops:
  8.0 1.2 copy-done
  9.2 4.7 fusion.6
  14.5 38.7 %all_to_all.63 = f32[2,64,8,256]{3,2,0,1:T(8,128)S(1)} all-to-all(f32[2,64,8,256]{3,2,0,1:T(8,128)S(1)} %copy.66), channel_id=1, replica_groups=mesh['tok'=64,'ch'=4] {'tok'}, dimensions={1} | all-to-all | bytes 2097152 | tf_op jit(solution)/shard_map/all_to_all | solution.py:19
  53.1 1.0 copy-done.4
  54.1 1.9 convolution_bitcast_fusion.5
  56.0 1.4 copy.68
  57.4 8.1 %all-to-all-start.1 = ((f32[128,8,256]{2,1,0:T(8,128)}), f32[128,8,256]{2,1,0:T(8,128)S(1)}, u32[]{:S(2)}, u32[]{:S(2)}) async-start(f32[128,8,256]{2,1,0:T(8,128)} %copy.68), calls=%async_computation.1 | async-start | bytes 2097152 | tf_op jit(solution)/shard_map/all_to_all | solution.py:29
  65.6 72.8 %all_gather.6 = bf16[1,256,1024]{2,0,1:T(2,128)(2,1)} all-gather(bf16[1,4,1024]{2,0,1:T(2,128)(2,1)S(1)} %copy.70), channel_id=1, replica_groups=mesh['tok'=64,'ch'=4] {'tok'}, dimensions={1}, use_global_device_ids=true | all-gather | bytes 532480 | tf_op jit(solution)/shard_map/all_gather | solution.py:38
  138.4 53.1 %all_gather.7 = bf16[1,1024,256]{2,1,0:T(8,128)(2,1)} all-gather(bf16[1,16,256]{2,1,0:T(8,128)(2,1)S(1)} %copy-done.11), channel_id=1, replica_groups=mesh['tok'=64,'ch'=4] {'tok'}, dimensions={1}, use_global_device_ids=true | all-gather | bytes 532480 | tf_op jit(solution)/shard_map/all_gather | solution.py:39
  191.6 1.0 copy-done.2
  193.1 2.4 multiply_convert_fusion
  195.4 2.2 fusion.5
  197.6 1.8 fusion.33
  199.5 35.5 %all_to_all.64 = f32[2,64,8,256]{3,2,0,1:T(8,128)S(1)} all-to-all(f32[2,64,8,256]{3,2,0,1:T(8,128)S(1)} %copy.71), channel_id=1, replica_groups=mesh['tok'=64,'ch'=4] {'tok'}, dimensions={1} | all-to-all | bytes 2097152 | tf_op jit(solution)/shard_map/all_to_all | solution.py:19
  235.1 1.1 copy-done.5
  236.1 2.9 convolution_bitcast_fusion.4
  239.0 2.7 copy.73
  241.7 8.3 %all-to-all-start.3 = ((f32[128,8,256]{2,1,0:T(8,128)}), f32[128,8,256]{2,1,0:T(8,128)}, u32[]{:S(2)}, u32[]{:S(2)}) async-start(f32[128,8,256]{2,1,0:T(8,128)} %copy.73), calls=%async_computation.3 | async-start | bytes 2097152 | tf_op jit(solution)/shard_map/all_to_all | solution.py:29
  250.0 3.3 convolution_bitcast_fusion.1
  253.4 3.6 convolution_bitcast_fusion
  258.6 3.4 convolution_add_fusion.1
  261.9 181.6 %all-reduce.5.cloned.1.call-done = f32[1,256,1024]{2,1,0:T(8,128)} async-done(((f32[1,256,1024]{2,1,0:T(8,128)}), f32[1,256,1024]{2,1,0:T(8,128)}) %all-reduce.5.cloned.1.call-update) | async-done | bytes 1048592
  443.6 1.4 constant_dynamic-slice_fusion
  444.9 3.6 convolution_bitcast_fusion.6
  448.6 4.2 convolution_bitcast_fusion.2
  452.8 4.4 convolution_bitcast_fusion.3
  457.2 2.6 copy.76
  459.7 2.9 fusion.10
  462.7 121.8 %reduce-scatter.3.cloned.1.call-done = f32[1,16,256]{2,1,0:T(8,128)} async-done(((f32[1,1024,256]{2,1,0:T(8,128)}), f32[1,16,256]{2,1,0:T(8,128)}) %reduce-scatter.3.cloned.1.call-update) | async-done | bytes 16400 | tf_op jit(solution)/shard_map/reduce_scatter | solution.py:64
  584.5 123.4 %all-reduce.7.cloned.1.call-done = (f32[512,512]{1,0:T(8,128)}, f32[128,128]{1,0:T(8,128)}) async-done(((f32[512,512]{1,0:T(8,128)}, f32[128,128]{1,0:T(8,128)}), (f32[512,512]{1,0:T(8,128)}, f32[128,128]{1,0:T(8,128)})) %all-reduce.7.cloned.1.call-update) | async-done | bytes 1114128 | tf_op jit(solution)/shard_map/psum | solution.py:75
  707.8 2.3 copy.110
  710.1 1.5 copy.111
  (41 shorter events, 2.2 us)
Async XLA Ops:
  8.0 1.2 copy-start
  9.2 44.9 %copy-start.9 = (f32[128,128]{1,0:T(8,128)S(1)}, f32[128,128]{1,0:T(8,128)}, u32[]{:S(2)}) copy-start(f32[128,128]{1,0:T(8,128)} %param.10) | copy-start | bytes 196612
  14.5 51.1 %copy-start.12 = (bf16[1,4,1024]{2,1,0:T(4,128)(2,1)S(1)}, bf16[1,4,1024]{2,1,0:T(4,128)(2,1)}, u32[]{:S(2)}) copy-start(bf16[1,4,1024]{2,1,0:T(4,128)(2,1)} %param.11) | copy-start | bytes 24580
  53.1 1.0 copy-start.4
  53.1 85.3 %copy-start.11 = (bf16[1,16,256]{2,1,0:T(8,128)(2,1)S(1)}, bf16[1,16,256]{2,1,0:T(8,128)(2,1)}, u32[]{:S(2)}) copy-start(bf16[1,16,256]{2,1,0:T(8,128)(2,1)} %param.12) | copy-start | bytes 24580
  56.0 136.5 %copy-start.1 = (f32[1024,256]{1,0:T(8,128)S(1)}, f32[1024,256]{1,0:T(8,128)}, u32[]{:S(2)}) copy-start(f32[1024,256]{1,0:T(8,128)} %param.7) | copy-start | bytes 3145732
  57.4 134.0 %all-to-all-start.1 = ((f32[128,8,256]{2,1,0:T(8,128)}), f32[128,8,256]{2,1,0:T(8,128)S(1)}, u32[]{:S(2)}, u32[]{:S(2)}) async-start(f32[128,8,256]{2,1,0:T(8,128)} %copy.68), calls=%async_computation.1 | async-start | bytes 2097152 | tf_op jit(solution)/shard_map/all_to_all | solution.py:29
  191.5 1.6 copy-start.6
  191.6 1.0 copy-start.2
  193.1 2.4 copy-start.8
  193.1 2.4 copy-start.13
  197.6 1.8 copy-start.7
  235.1 1.1 copy-start.5
  241.7 206.9 %all-to-all-start.3 = ((f32[128,8,256]{2,1,0:T(8,128)}), f32[128,8,256]{2,1,0:T(8,128)}, u32[]{:S(2)}, u32[]{:S(2)}) async-start(f32[128,8,256]{2,1,0:T(8,128)} %copy.73), calls=%async_computation.3 | async-start | bytes 2097152 | tf_op jit(solution)/shard_map/all_to_all | solution.py:29
  250.0 193.6 %all-reduce.5.cloned.1.call-start = ((), (), s32[]{:S(2)}) async-start(), calls=%async_computation.6 | async-start | bytes 2097152
  253.3 4.0 copy-start.14
  253.4 331.1 %reduce-scatter.3.cloned.1.call-start = ((), (), s32[]{:S(2)}) async-start(), calls=%async_computation.5 | async-start | bytes 1064960 | tf_op jit(solution)/shard_map/reduce_scatter | solution.py:64
  257.0 450.8 %all-reduce.7.cloned.1.call-start = ((), (), s32[]{:S(2)}) async-start(), calls=%async_computation.7 | async-start | bytes 2228224 | tf_op jit(solution)/shard_map/psum | solution.py:75
  258.5 190.0 %copy-start.10 = (f32[2,512]{1,0:T(2,128)S(1)}, f32[2,512]{1,0:T(2,128)}, u32[]{:S(2)}) copy-start(f32[2,512]{1,0:T(2,128)} %param.9) | copy-start | bytes 12292
  448.6 11.2 %copy-start.3 = (f32[2,64,8,256]{3,2,1,0:T(8,128)S(1)}, f32[2,64,8,256]{3,2,1,0:T(8,128)}, u32[]{:S(2)}) copy-start(f32[2,64,8,256]{3,2,1,0:T(8,128)} %copy-done.2) | copy-start | bytes 3145732
Sparse Core Ops, SparseCore 0:
  255.2 188.3 all-reduce.4
  448.1 136.2 reduce-scatter.2
Sparse Core Ops, SparseCore 1:
  452.9 254.9 all-reduce.6
where the time goes:
time: 720 us; the launch traced here: 719 us
  waiting for transfers between devices  427 us (59%)
  blocking collectives  200 us (28%)
  matrix products  38.3 us (5%)
  local copies, waits for them, and re-layouts  17.5 us (2%)
  starting transfers between devices  16.7 us (2%)
  between operations  16.3 us (2%)
    unnamed x4, waiting for transfers between devices  182 us
    psum x1, waiting for transfers between devices, local(): grad_one, grad_two = lax.psum((one_part, two_part), ('tok', 'ch'))  123 us
    reduce_scatter x1, waiting for transfers between devices, local(): lax.psum_scatter(grad_down_part[None], 'tok', scatter_dimension=1, tiled=...  122 us
    all_to_all x2, blocking collectives, to_columns(): lax.all_to_all(block.reshape(rows, count, width // count, chans), 'tok',...  74.2 us
    all_gather x1, blocking collectives, local(): lax.all_gather(w_up, 'tok', axis=1, tiled=True)  72.8 us
    all_gather x1, blocking collectives, local(): lax.all_gather(w_down, 'tok', axis=1, tiled=True)  53.1 us
    all_to_all x2, starting transfers between devices, to_rows(): return lax.all_to_all(block, 'tok', split_axis=0, concat_axis=1, tiled=True)  16.4 us
  transfers between devices with their start and end apart: 5, of which 3 were waited for; matrix products, arithmetic and copies ran while one was open for 4% of the time, Pallas kernels for 0%

commit v1 on v0

--- a/solution.py
+++ b/solution.py
@@ -72,7 +72,7 @@
     one_part = jnp.einsum("ikc,ijc->kj", d_first, grid, precision=high)
     d_grid = jnp.einsum("kj,ikc->ijc", factor_one, d_first, precision=high)
     grad_inputs = direct + d_grid.reshape(rows * width, chans)
-    grad_one, grad_two = lax.psum((one_part, two_part), ("tok", "ch"))
+    grad_one, grad_two = lax.psum(lax.psum((one_part, two_part), "ch"), "tok")
     return (outputs, grad_inputs, grad_one, grad_two, grad_up, grad_down)
 
 

time: 720 us -> 679 us (0.943)
  waiting for transfers between devices: 427 us -> 387 us
    unnamed x4 -> x3, waiting for transfers between devices: 182 us -> 0.05 us
    psum x1 -> x2, waiting for transfers between devices: 123 us -> 223 us  [local(): grad_one, grad_two = lax.psum(lax.psum((one_part, two_part), 'ch'), 'tok')]
    all_to_all x2, waiting for transfers between devices: 0.01 us -> 22.7 us  [to_rows(): return lax.all_to_all(block, 'tok', split_axis=0, concat_axis=1, tiled=True)]
    reduce_scatter x1, waiting for transfers between devices: 122 us -> 141 us  [local(): lax.psum_scatter(grad_down_part[None], 'tok', scatter_dimension=1, tiled=...]
  transfers between devices with their start and end apart: 5 -> 5, of which waited for: 3 -> 4; matrix products, arithmetic and copies ran while one was open for 4% -> 4% of each run, Pallas kernels for 0% -> 0%
where the time goes in v1:
time: 679 us; the launch traced here: 678 us
  waiting for transfers between devices  387 us (57%)
  blocking collectives  200 us (29%)
  matrix products  38.3 us (6%)
  local copies, waits for them, and re-layouts  17.4 us (3%)
  starting transfers between devices  16.7 us (2%)
  between operations  14.6 us (2%)
    psum x2, waiting for transfers between devices, local(): grad_one, grad_two = lax.psum(lax.psum((one_part, two_part), 'ch'), 'tok')  223 us
    reduce_scatter x1, waiting for transfers between devices, local(): lax.psum_scatter(grad_down_part[None], 'tok', scatter_dimension=1, tiled=...  141 us
    all_to_all x2, blocking collectives, to_columns(): lax.all_to_all(block.reshape(rows, count, width // count, chans), 'tok',...  74.5 us
    all_gather x1, blocking collectives, local(): lax.all_gather(w_up, 'tok', axis=1, tiled=True)  72.8 us
    all_gather x1, blocking collectives, local(): lax.all_gather(w_down, 'tok', axis=1, tiled=True)  53 us
    all_to_all x2, waiting for transfers between devices, to_rows(): return lax.all_to_all(block, 'tok', split_axis=0, concat_axis=1, tiled=True)  22.7 us
    all_to_all x2, starting transfers between devices, to_rows(): return lax.all_to_all(block, 'tok', split_axis=0, concat_axis=1, tiled=True)  16.4 us
  transfers between devices with their start and end apart: 5, of which 4 were waited for; matrix products, arithmetic and copies ran while one was open for 4% of the time, Pallas kernels for 0%

profile of v1, /device:TPU:4, one launch (start us, length us, event | category | flops | bytes accessed | tf_op | source)
XLA Modules:
  0.0 677.7 jit_solution(5887727596190054974)
XLA Ops:
  7.2 1.2 copy-done
  8.4 4.7 fusion.6
  13.6 38.7 %all_to_all.63 = f32[2,64,8,256]{3,2,0,1:T(8,128)S(1)} all-to-all(f32[2,64,8,256]{3,2,0,1:T(8,128)S(1)} %copy.66), channel_id=1, replica_groups=mesh['tok'=64,'ch'=4] {'tok'}, dimensions={1} | all-to-all | bytes 2097152 | tf_op jit(solution)/shard_map/all_to_all | solution.py:19
  52.3 1.0 copy-done.4
  53.3 1.9 convolution_bitcast_fusion.5
  55.2 1.4 copy.68
  56.6 8.1 %all-to-all-start.1 = ((f32[128,8,256]{2,1,0:T(8,128)}), f32[128,8,256]{2,1,0:T(8,128)S(1)}, u32[]{:S(2)}, u32[]{:S(2)}) async-start(f32[128,8,256]{2,1,0:T(8,128)} %copy.68), calls=%async_computation.1 | async-start | bytes 2097152 | tf_op jit(solution)/shard_map/all_to_all | solution.py:29
  64.7 72.8 %all_gather.6 = bf16[1,256,1024]{2,0,1:T(2,128)(2,1)} all-gather(bf16[1,4,1024]{2,0,1:T(2,128)(2,1)S(1)} %copy.70), channel_id=1, replica_groups=mesh['tok'=64,'ch'=4] {'tok'}, dimensions={1}, use_global_device_ids=true | all-gather | bytes 532480 | tf_op jit(solution)/shard_map/all_gather | solution.py:38
  137.6 53.0 %all_gather.7 = bf16[1,1024,256]{2,1,0:T(8,128)(2,1)} all-gather(bf16[1,16,256]{2,1,0:T(8,128)(2,1)S(1)} %copy-done.11), channel_id=1, replica_groups=mesh['tok'=64,'ch'=4] {'tok'}, dimensions={1}, use_global_device_ids=true | all-gather | bytes 532480 | tf_op jit(solution)/shard_map/all_gather | solution.py:39
  190.6 1.0 copy-done.2
  192.1 2.4 multiply_convert_fusion
  194.5 2.2 fusion.5
  196.7 1.8 fusion.33
  198.6 35.8 %all_to_all.64 = f32[2,64,8,256]{3,2,0,1:T(8,128)S(1)} all-to-all(f32[2,64,8,256]{3,2,0,1:T(8,128)S(1)} %copy.71), channel_id=1, replica_groups=mesh['tok'=64,'ch'=4] {'tok'}, dimensions={1} | all-to-all | bytes 2097152 | tf_op jit(solution)/shard_map/all_to_all | solution.py:19
  235.4 2.9 convolution_bitcast_fusion.4
  238.3 2.6 copy.73
  240.9 8.3 %all-to-all-start.3 = ((f32[128,8,256]{2,1,0:T(8,128)}), f32[128,8,256]{2,1,0:T(8,128)}, u32[]{:S(2)}, u32[]{:S(2)}) async-start(f32[128,8,256]{2,1,0:T(8,128)} %copy.73), calls=%async_computation.3 | async-start | bytes 2097152 | tf_op jit(solution)/shard_map/all_to_all | solution.py:29
  249.4 3.6 convolution_bitcast_fusion.6
  253.1 22.7 %all-to-all-done.3 = f32[128,8,256]{2,1,0:T(8,128)} async-done(((f32[128,8,256]{2,1,0:T(8,128)}), f32[128,8,256]{2,1,0:T(8,128)}, u32[]{:S(2)}, u32[]{:S(2)}) %all-to-all-start.3) | async-done | bytes 1048608 | tf_op jit(solution)/shard_map/all_to_all | solution.py:29
  275.7 4.1 convolution_bitcast_fusion.2
  279.9 3.3 convolution_bitcast_fusion.1
  283.2 47.1 %all-reduce.8.cloned.1.call-done = (f32[512,512]{1,0:T(8,128)}, f32[128,128]{1,0:T(8,128)}) async-done(((f32[512,512]{1,0:T(8,128)}, f32[128,128]{1,0:T(8,128)}), (f32[512,512]{1,0:T(8,128)}, f32[128,128]{1,0:T(8,128)})) %all-reduce.8.cloned.1.call-update) | async-done | bytes 1114128 | tf_op jit(solution)/shard_map/psum | solution.py:75
  330.4 3.7 convolution_bitcast_fusion
  335.3 3.4 convolution_add_fusion.1
  338.7 4.5 convolution_bitcast_fusion.3
  343.2 2.6 copy.76
  345.8 2.9 fusion.10
  348.7 175.9 %all-reduce.6.cloned.1.call-done = (f32[512,512]{1,0:T(8,128)}, f32[128,128]{1,0:T(8,128)}, f32[1,256,1024]{2,1,0:T(8,128)}) async-done(((f32[512,512]{1,0:T(8,128)}, f32[128,128]{1,0:T(8,128)}, f32[1,256,1024]{2,1,0:T(8,128)}), (f32[512,512]{1,0:T(8,128)}, f32[128,128]{1,0:T(8,128)}, f32[1,256,1024]{2,1,0:T(8,128)})) %all-reduce.6.cloned.1.call-update) | async-done | bytes 2162704 | tf_op jit(solution)/shard_map/psum | solution.py:75
  524.6 1.4 constant_dynamic-slice_fusion
  526.0 141.4 %reduce-scatter.3.cloned.1.call-done = f32[1,16,256]{2,1,0:T(8,128)} async-done(((f32[1,1024,256]{2,1,0:T(8,128)}), f32[1,16,256]{2,1,0:T(8,128)}) %reduce-scatter.3.cloned.1.call-update) | async-done | bytes 16400 | tf_op jit(solution)/shard_map/reduce_scatter | solution.py:64
  667.4 2.3 copy.112
  669.7 1.5 copy.113
  (41 shorter events, 3.2 us)
Async XLA Ops:
  7.2 1.2 copy-start
  8.4 44.9 %copy-start.9 = (f32[128,128]{1,0:T(8,128)S(1)}, f32[128,128]{1,0:T(8,128)}, u32[]{:S(2)}) copy-start(f32[128,128]{1,0:T(8,128)} %param.10) | copy-start | bytes 196612
  13.6 51.1 %copy-start.12 = (bf16[1,4,1024]{2,1,0:T(4,128)(2,1)S(1)}, bf16[1,4,1024]{2,1,0:T(4,128)(2,1)}, u32[]{:S(2)}) copy-start(bf16[1,4,1024]{2,1,0:T(4,128)(2,1)} %param.11) | copy-start | bytes 24580
  52.3 1.0 copy-start.4
  52.3 85.3 %copy-start.11 = (bf16[1,16,256]{2,1,0:T(8,128)(2,1)S(1)}, bf16[1,16,256]{2,1,0:T(8,128)(2,1)}, u32[]{:S(2)}) copy-start(bf16[1,16,256]{2,1,0:T(8,128)(2,1)} %param.12) | copy-start | bytes 24580
  55.2 136.4 %copy-start.1 = (f32[1024,256]{1,0:T(8,128)S(1)}, f32[1024,256]{1,0:T(8,128)}, u32[]{:S(2)}) copy-start(f32[1024,256]{1,0:T(8,128)} %param.7) | copy-start | bytes 3145732
  56.6 133.9 %all-to-all-start.1 = ((f32[128,8,256]{2,1,0:T(8,128)}), f32[128,8,256]{2,1,0:T(8,128)S(1)}, u32[]{:S(2)}, u32[]{:S(2)}) async-start(f32[128,8,256]{2,1,0:T(8,128)} %copy.68), calls=%async_computation.1 | async-start | bytes 2097152 | tf_op jit(solution)/shard_map/all_to_all | solution.py:29
  190.5 1.6 copy-start.6
  190.6 1.0 copy-start.2
  192.1 2.4 copy-start.8
  192.1 2.4 copy-start.13
  196.7 1.8 copy-start.7
  234.4 1.0 copy-start.5
  235.4 40.3 %copy-start.10 = (f32[2,512]{1,0:T(2,128)S(1)}, f32[2,512]{1,0:T(2,128)}, u32[]{:S(2)}) copy-start(f32[2,512]{1,0:T(2,128)} %param.9) | copy-start | bytes 12292
  240.9 34.9 %all-to-all-start.3 = ((f32[128,8,256]{2,1,0:T(8,128)}), f32[128,8,256]{2,1,0:T(8,128)}, u32[]{:S(2)}, u32[]{:S(2)}) async-start(f32[128,8,256]{2,1,0:T(8,128)} %copy.73), calls=%async_computation.3 | async-start | bytes 2097152 | tf_op jit(solution)/shard_map/all_to_all | solution.py:29
  249.2 81.1 %all-reduce.8.cloned.1.call-start = ((), (), s32[]{:S(2)}) async-start(), calls=%async_computation.7 | async-start | bytes 2228224 | tf_op jit(solution)/shard_map/psum | solution.py:75
  279.9 244.8 %all-reduce.6.cloned.1.call-start = ((), (), s32[]{:S(2)}) async-start(), calls=%async_computation.6 | async-start | bytes 4325376 | tf_op jit(solution)/shard_map/psum | solution.py:75
  330.3 3.8 copy-start.14
  330.3 337.1 %reduce-scatter.3.cloned.1.call-start = ((), (), s32[]{:S(2)}) async-start(), calls=%async_computation.5 | async-start | bytes 1064960 | tf_op jit(solution)/shard_map/reduce_scatter | solution.py:64
  338.7 7.1 %copy-start.3 = (f32[2,64,8,256]{3,2,1,0:T(8,128)S(1)}, f32[2,64,8,256]{3,2,1,0:T(8,128)}, u32[]{:S(2)}) copy-start(f32[2,64,8,256]{3,2,1,0:T(8,128)} %copy-done.2) | copy-start | bytes 3145732
Sparse Core Ops, SparseCore 0:
  280.0 50.2 all-reduce.7
  334.4 190.1 all-reduce.5
  529.7 137.6 reduce-scatter.2
